TPU v7x, 32 devices: a whole 2x2x4 slice. The times are simulated.
32 devices in a mesh: seq: 16 (over z, y, x), head: 2 (over core).
Axes of the slice: x: 2, y: 2, z: 4, core: 2. Of those that a mesh axis runs over, the one named last changes fastest.
Arguments:
- raw_keys: bfloat16 [2, 16384, 8, 128], P(None, 'seq', 'head'), may hold values from -6 to 6
- raw_values: bfloat16 [2, 16384, 8, 128], P(None, 'seq', 'head'), may hold values from -6 to 6
- phase: int32 [2], replicated, may hold values from 0 to 255, as said below
- ratio: int32 [2, 16], replicated, may hold values from 8 to 32, as said below
- resident_len: int32 [2, 16], replicated, may hold values from 1 to 256, as said below
- beacon_queries: bfloat16 [2, 2048, 8, 8, 128], P(None, 'seq', 'head'), may hold values from -150 to 150
- beacon_wk: bfloat16 [8192, 1024], P('seq', 'head'), may hold values from -0.125 to 0.125
- beacon_wv: bfloat16 [8192, 1024], P('seq', 'head'), may hold values from -0.125 to 0.125
- resident_keys: bfloat16 [2, 4096, 8, 128], P(None, 'seq', 'head'), may hold values from -6 to 6
- resident_values: bfloat16 [2, 4096, 8, 128], P(None, 'seq', 'head'), may hold values from -6 to 6
- decode_queries: bfloat16 [4, 2, 8, 8, 128], P(None, None, 'head'), may hold values from -150 to 150
- out_weight: bfloat16 [8192, 8192], P('head', 'seq'), may hold values from -0.0625 to 0.0625
Outputs:
- beacon_keys: bfloat16 [2, 2048, 8, 128], P(None, 'seq', 'head')
- beacon_values: bfloat16 [2, 2048, 8, 128], P(None, 'seq', 'head')
- projected: bfloat16 [4, 2, 8192], P(None, None, 'seq')
Inputs may be any that keep to these rules, and one draw needn't show every extreme that they name: `phase`: some request has 255. `ratio`: each value is 1024 // 128 times 1, 2 or 4; both ends occur. `resident_len`: some pair has 256.
All inputs are finite; a program needn't handle non-finite values.
Results may differ from a plain program's by a relative error of at most 0.025.
Values may be sent and summed in bfloat16 or wider, within the bound.
A program may use at most 64 MiB of HBM per device.

v0:
```python
import math

import jax
import jax.numpy as jnp
from jax import lax
from jax.sharding import PartitionSpec as P

G = 8
INTERVAL = 1024
NB = 128
OFF = 256
STEPS = 4


masked_score = -1e30


def shifted(value, axis, steps):
    count = lax.axis_size(axis)
    first, last = (max(0, -steps), min(count, count - steps))
    return lax.ppermute(value, axis, [(source, source + steps) for source in range(first, last)])


def joined(shard, axis, combine):
    everything = jax.tree.map(lambda part: lax.all_gather(part, axis), shard)
    first = jax.tree.map(lambda part: part[0], everything)

    def hop(k, so_far):
        return combine(so_far, jax.tree.map(lambda part: part[k], everything))

    return lax.fori_loop(1, lax.axis_size(axis), hop, first)


def blend(former, latter):
    row_peak = jnp.maximum(former[0], latter[0])
    former_scale = jnp.exp(former[0] - row_peak)
    latter_scale = jnp.exp(latter[0] - row_peak)
    weight_sum = former[1] * former_scale + latter[1] * latter_scale
    weighted = former[2] * former_scale[..., None] + latter[2] * latter_scale[..., None]
    return (row_peak, weight_sum, weighted)


def pool_part(queries, key_rows, value_rows, positions, present, reaches):
    inv_root = 1.0 / math.sqrt(queries.shape[-1])

    def per_request(members):
        query_block, key_block, value_block, position_row, present_row, reach_row = members
        scores = (
            jnp.einsum("jkgd,ikd->jkgi", query_block, key_block, preferred_element_type=jnp.float32)
            * inv_root
        )
        allowed = (
            present_row[None, :]
            & (position_row[None, :] >= 0)
            & (position_row[None, :] < INTERVAL)
            & (position_row[None, :] < reach_row[:, None])
        )
        cache_mask = allowed[:, None, None, :]
        row_peak = jnp.max(jnp.where(cache_mask, scores, masked_score), axis=-1)
        weights = jnp.where(cache_mask, jnp.exp(scores - row_peak[..., None]), 0.0)
        weight_sum = jnp.sum(weights, axis=-1)
        weighted = jnp.einsum(
            "jkgi,ikd->jkgd",
            weights.astype(jnp.bfloat16),
            value_block,
            preferred_element_type=jnp.float32,
        )
        return (row_peak, weight_sum, weighted)

    return lax.map(per_request, (queries, key_rows, value_rows, positions, present, reaches))


def body(
    raw_keys,
    raw_values,
    phase,
    ratio,
    resident_len,
    beacon_queries,
    beacon_wk,
    beacon_wv,
    resident_keys,
    resident_values,
    decode_queries,
    out_weight,
):
    requests = raw_keys.shape[0]
    kv_local = raw_keys.shape[2]
    head_dim = raw_keys.shape[3]
    shard_index = lax.axis_index("seq")
    shard_count = lax.axis_size("seq")
    is_first = shard_index == 0
    is_last = shard_index == shard_count - 1
    own_ratio = lax.dynamic_index_in_dim(ratio, shard_index, 1, keepdims=False)
    slot_ids = jnp.arange(NB, dtype=jnp.int32)
    lead_in = jnp.where(is_first, phase, 0)
    reaches = (slot_ids[None, :] + 1) * own_ratio[:, None] + lead_in[:, None]
    tail_keys = raw_keys[:, INTERVAL - OFF :]
    tail_values = raw_values[:, INTERVAL - OFF :]
    own_positions = jnp.arange(INTERVAL, dtype=jnp.int32)[None, :] + phase[:, None]
    rim_ids = jnp.arange(OFF, dtype=jnp.int32)
    rim_positions = rim_ids[None, :] - OFF + phase[:, None]
    near_keys, near_values = shifted((tail_keys, tail_values), "seq", 1)
    key_rows = jnp.concatenate([near_keys, raw_keys], axis=1)
    value_rows = jnp.concatenate([near_values, raw_values], axis=1)
    positions = jnp.concatenate([rim_positions, own_positions], axis=1)
    present = jnp.logical_not(is_first) | (positions >= phase[:, None])
    pooled_parts = pool_part(beacon_queries, key_rows, value_rows, positions, present, reaches)
    pooled = (pooled_parts[2] / pooled_parts[1][..., None]).astype(jnp.bfloat16)
    pooled_flat = pooled.reshape(requests * NB, kv_local * G * head_dim)
    pooled_whole = lax.all_gather(pooled_flat, "head", axis=1, tiled=True)
    key_sum = jnp.dot(
        pooled_whole,
        lax.all_gather(beacon_wk, "seq", axis=0, tiled=True),
        preferred_element_type=jnp.float32,
    )
    value_sum = jnp.dot(
        pooled_whole,
        lax.all_gather(beacon_wv, "seq", axis=0, tiled=True),
        preferred_element_type=jnp.float32,
    )
    made_keys = key_sum
    made_values = value_sum
    made_keys = made_keys.reshape(requests, NB, kv_local, head_dim)
    made_values = made_values.reshape(requests, NB, kv_local, head_dim)
    slot_live = slot_ids[None, :] < (INTERVAL // own_ratio)[:, None]
    beacon_keys = jnp.where(slot_live[:, :, None, None], made_keys, 0.0).astype(jnp.bfloat16)
    beacon_values = jnp.where(slot_live[:, :, None, None], made_values, 0.0).astype(jnp.bfloat16)
    cache_keys = jnp.concatenate([resident_keys, beacon_keys, tail_keys], axis=1)
    cache_values = jnp.concatenate([resident_values, beacon_values, tail_values], axis=1)
    own_len = lax.dynamic_index_in_dim(resident_len, shard_index, 1, keepdims=False)
    resident_ok = jnp.arange(resident_keys.shape[1], dtype=jnp.int32)[None, :] < own_len[:, None]
    leftover_ok = (rim_ids[None, :] >= OFF - phase[:, None]) & is_last
    usable = jnp.concatenate([resident_ok, slot_live, leftover_ok], axis=1)
    inv_root = 1.0 / math.sqrt(head_dim)
    scores = (
        jnp.einsum(
            "srkgd,rikd->rksgi", decode_queries, cache_keys, preferred_element_type=jnp.float32
        )
        * inv_root
    )
    cache_mask = usable[:, None, None, None, :]
    row_peak = jnp.max(jnp.where(cache_mask, scores, masked_score), axis=-1)
    weights = jnp.where(cache_mask, jnp.exp(scores - row_peak[..., None]), 0.0)
    weight_sum = jnp.sum(weights, axis=-1)
    weighted = jnp.einsum(
        "rksgi,rikd->rksgd",
        weights.astype(jnp.bfloat16),
        cache_values,
        preferred_element_type=jnp.float32,
    )
    merged = joined((row_peak, weight_sum, weighted), "seq", blend)
    total_sum = merged[1]
    total_weighted = merged[2]
    attended = (total_weighted / total_sum[..., None]).astype(jnp.bfloat16)
    attended = jnp.transpose(attended, (2, 0, 1, 3, 4)).reshape(
        STEPS * requests, kv_local * G * head_dim
    )
    partial_value = jnp.dot(attended, out_weight, preferred_element_type=jnp.float32)
    summed = lax.psum(partial_value, "head")
    projected = summed.astype(jnp.bfloat16).reshape(STEPS, requests, out_weight.shape[1])
    return (beacon_keys, beacon_values, projected)


def solution(mesh):
    return jax.shard_map(
        body,
        mesh=mesh,
        in_specs=(
            P(None, "seq", "head", None),
            P(None, "seq", "head", None),
            P(),
            P(),
            P(),
            P(None, "seq", "head", None, None),
            P("seq", "head"),
            P("seq", "head"),
            P(None, "seq", "head", None),
            P(None, "seq", "head", None),
            P(None, None, "head", None, None),
            P("head", "seq"),
        ),
        out_specs=(
            P(None, "seq", "head", None),
            P(None, "seq", "head", None),
            P(None, None, "seq"),
        ),
        check_vma=False,
    )
```

profile of v0, /device:TPU:0, one launch (start us, length us, event | category | flops | bytes accessed | tf_op | source)
XLA Modules:
  0.0 473.2 jit_solution(14405717227986694837)
XLA Ops:
  7.2 1.9 copy.46
  9.2 0.9 slice.23
  10.1 4.9 %collective-permute-start = (bf16[2,256,4,128]{3,1,2,0:T(8,128)(2,1)}, bf16[2,256,4,128]{3,1,2,0:T(8,128)(2,1)S(1)}, u32[]{:S(2)}, u32[]{:S(2)}) collective-permute-start(bf16[2,256,4,128]{3,1,2,0:T(8,128)(2,1)} %slice.23), channel_id=1, source_target_pairs={{0,2},{2,4},{4,6},{6,8},{8,10},{10,12},{12,14},{14,16},{16,18},{18... | collective-permute-start | bytes 1572872 | tf_op jit(solution)/shard_map/ppermute | solution.py:21
  15.0 0.9 copy.67
  15.8 4.2 collective-permute-start.1
  20.1 4.4 copy.50
  24.5 0.3 fusion.39
  24.9 0.1 compare_or_fusion
  25.0 12.6 %collective-permute-done.1 = bf16[2,256,4,128]{3,1,2,0:T(8,128)(2,1)} collective-permute-done((bf16[2,256,4,128]{3,1,2,0:T(8,128)(2,1)}, bf16[2,256,4,128]{3,1,2,0:T(8,128)(2,1)}, u32[]{:S(2)}, u32[]{:S(2)}) %collective-permute-start.1) | collective-permute-done | bytes 524320 | tf_op jit(solution)/shard_map/ppermute | solution.py:21
  37.6 1.2 copy.49
  38.9 3.2 pad_maximum_fusion.1
  42.1 1.7 pad_maximum_fusion
  43.8 51.0 %while.31 = (s32[]{:T(128)}, f32[2,128,4,8]{1,3,2,0:T(8,128)S(1)}, f32[2,128,4,8,128]{1,4,3,2,0:T(8,128)}, pred[2,1280]{1,0:T(4,128)(4,1)S(1)}, s32[2,1280]{1,0:...) while((s32[]{:T(128)}, f32[2,128,4,8]{1,3,2,0:T(8,128)S(1)}, ...), condition=%wide.region_3.4_spmd, body=%wide.region_0.3_spmd.sunk | while | flops 2716145920 | bytes 71183224 | solution.py:70
  43.9 0.9 compare_and_fusion.3
  44.9 1.3 constant_dynamic-slice_fusion.3
  46.2 4.2 convolution_multiply_fusion.2
  50.4 11.6 %fusion.66 = (f32[128,4,8]{0,2,1:T(8,128)S(1)}, bf16[128,4,8,1280]{0,3,2,1:T(8,128)(2,1)}) fusion(f32[4,1280,128,8]{2,1,3,0:T(8,128)S(1)} %convolution_multiply_fusion.2, pred[128,1280]{0,1:T(8,128)(4,1)S(1)} %compare_and_fusion.3), kind=kOutput, calls=%fused_computation.85.clone.1 | output fusion | flops 26215680 | bytes 31637504 | tf_op jit(solution)/shard_map/while/body/eval_jaxpr/sub | solution.py:60
  62.1 7.3 %bitcast_dynamic-update-slice_fusion.5 = f32[2,128,4,8,128]{1,4,3,2,0:T(8,128)} fusion(f32[2,128,4,8,128]{1,4,3,2,0:T(8,128)} %get-tuple-element.439, s32[]{:T(128)} %get-tuple-element.437, bf16[128,4,8,1280]{0,3,2,1:T(8,128)(2,1)} %get-tuple-element.415, bf16[2,1280,4,128]{1,3,2,0:T(8,128)(2,1)} %get-tuple-element.455), kind=kOutput, calls=%fused_computation.19.clone.1 | convolution fusion | flops 1342177280 | bytes 13894656 | tf_op jit(solution)/shard_map/while/body/eval_jaxpr/jkgi,ikd->jkgd/dot_general | solution.py:62
  69.4 0.9 compare_and_fusion.3
  70.4 1.3 constant_dynamic-slice_fusion.3
  71.7 4.2 convolution_multiply_fusion.2
  75.9 11.6 %fusion.66 = (f32[128,4,8]{0,2,1:T(8,128)S(1)}, bf16[128,4,8,1280]{0,3,2,1:T(8,128)(2,1)}) fusion(f32[4,1280,128,8]{2,1,3,0:T(8,128)S(1)} %convolution_multiply_fusion.2, pred[128,1280]{0,1:T(8,128)(4,1)S(1)} %compare_and_fusion.3), kind=kOutput, calls=%fused_computation.85.clone.1 | output fusion | flops 26215680 | bytes 31637504 | tf_op jit(solution)/shard_map/while/body/eval_jaxpr/sub | solution.py:60
  87.5 7.3 %bitcast_dynamic-update-slice_fusion.5 = f32[2,128,4,8,128]{1,4,3,2,0:T(8,128)} fusion(f32[2,128,4,8,128]{1,4,3,2,0:T(8,128)} %get-tuple-element.439, s32[]{:T(128)} %get-tuple-element.437, bf16[128,4,8,1280]{0,3,2,1:T(8,128)(2,1)} %get-tuple-element.415, bf16[2,1280,4,128]{1,3,2,0:T(8,128)(2,1)} %get-tuple-element.455), kind=kOutput, calls=%fused_computation.19.clone.1 | convolution fusion | flops 1342177280 | bytes 13894656 | tf_op jit(solution)/shard_map/while/body/eval_jaxpr/jkgi,ikd->jkgd/dot_general | solution.py:62
  94.8 2.8 divide_convert_fusion
  97.6 3.0 copy.52
  100.6 4.3 reshape.105
  104.9 0.2 all-gather.10.cloned.1.call-start
  105.1 0.5 all-gather.10.cloned.1.call-update
  105.7 0.7 all-gather.12.cloned.1.call-update
  106.7 0.1 compare_and_fusion.1
  106.8 14.1 %all-gather.8.cloned.1.call-done = bf16[256,8192]{1,0:T(8,128)(2,1)} async-done(((bf16[256,4096]{1,0:T(8,128)(2,1)}), bf16[256,8192]{1,0:T(8,128)(2,1)}) %all-gather.8.cloned.1.call-update) | async-done | bytes 4194320 | tf_op jit(solution)/shard_map/all_gather | solution.py:111
  120.9 116.3 %all-gather.10.cloned.1.call-done = bf16[8192,512]{1,0:T(8,128)(2,1)} async-done(((bf16[512,512]{1,0:T(8,128)(2,1)}), bf16[8192,512]{1,0:T(8,128)(2,1)}) %all-gather.10.cloned.1.call-update) | async-done | bytes 8388624 | tf_op jit(solution)/shard_map/all_gather | solution.py:114
  237.2 7.0 %fusion.45 = bf16[256,512]{1,0:T(8,128)(2,1)S(1)} fusion(bf16[256,8192]{1,0:T(8,128)(2,1)} %all-gather.8.cloned.1.call-done, bf16[8192,512]{1,0:T(8,128)(2,1)} %all-gather.10.cloned.1.call-done), kind=kOutput, calls=%fused_computation.86 | convolution fusion | flops 2147483648 | bytes 12845056 | tf_op jit(solution)/shard_map/dot_general | solution.py:112
  244.3 106.2 %all-gather.12.cloned.1.call-done = bf16[8192,512]{1,0:T(8,128)(2,1)} async-done(((bf16[512,512]{1,0:T(8,128)(2,1)}), bf16[8192,512]{1,0:T(8,128)(2,1)}) %all-gather.12.cloned.1.call-update) | async-done | bytes 8388624 | tf_op jit(solution)/shard_map/all_gather | solution.py:119
  350.5 7.0 %fusion.46 = bf16[256,512]{1,0:T(8,128)(2,1)S(1)} fusion(bf16[256,8192]{1,0:T(8,128)(2,1)} %all-gather.8.cloned.1.call-done, bf16[8192,512]{1,0:T(8,128)(2,1)} %all-gather.12.cloned.1.call-done), kind=kOutput, calls=%fused_computation.87 | convolution fusion | flops 2147483648 | bytes 12845056 | tf_op jit(solution)/shard_map/dot_general | solution.py:117
  357.6 0.2 fusion.32
  357.8 1.7 select_reduce_fusion
  359.5 2.1 fusion.26
  361.6 0.9 copy.59
  362.5 0.9 copy.60
  363.4 0.3 bitcast_reduce_fusion
  363.7 39.8 %all-gather.1 = f32[32,4,4,8]{3,2,1,0:T(4,128)S(1)} all-gather(f32[2,4,4,8]{3,2,1,0:T(4,128)S(1)} %bitcast_reduce_fusion), channel_id=3, replica_groups=mesh['seq'=16,'head'=2] {'seq'}, dimensions={0}, use_global_device_ids=true | all-gather | bytes 17408 | tf_op jit(solution)/shard_map/all_gather | solution.py:25
  403.5 38.1 %all-gather = f32[32,4,4,8]{3,2,1,0:T(4,128)S(1)} all-gather(f32[2,4,4,8]{3,2,1,0:T(4,128)S(1)} %get-tuple-element.312), channel_id=2, replica_groups=mesh['seq'=16,'head'=2] {'seq'}, dimensions={0}, use_global_device_ids=true | all-gather | bytes 17408 | tf_op jit(solution)/shard_map/all_gather | solution.py:25
  441.7 0.9 slice.26
  442.6 17.0 %while.32 = (s32[]{:T(128)}, f32[2,4,4,8]{3,2,1,0:T(4,128)S(1)}, f32[2,4,4,8]{3,2,1,0:T(4,128)S(1)}, f32[2,4,4,8,128]{4,3,2,1,0:T(8,128)S(1)}, f32[16,2,4,4,8]{4...) while((s32[]{:T(128)}, f32[2,4,4,8]{3,2,1,0:T(4,128)S(1)}, ...), condition=%wide.region_7.8_spmd, body=%wide.region_6.7_spmd.sunk | while | flops 99845 | bytes 403607 | solution.py:31
  442.6 1.1 fusion.68
  443.8 1.1 fusion.68
  444.9 1.1 fusion.68
  446.1 1.1 fusion.68
  447.2 1.1 fusion.68
  448.3 1.1 fusion.68
  449.5 1.1 fusion.68
  450.6 1.1 fusion.68
  451.7 1.1 fusion.68
  452.9 1.1 fusion.68
  454.0 1.1 fusion.68
  455.1 1.1 fusion.68
  456.3 1.1 fusion.68
  457.4 1.1 fusion.68
  458.5 1.1 fusion.68
  459.6 0.1 fusion.38
  459.8 2.8 fusion.47
  462.6 3.4 psum.7
  466.0 0.6 reshape.109
  (64 shorter events, 1.6 us)
Async XLA Ops:
  7.2 350.6 %copy-start = (bf16[4,2,4,8,128]{4,3,2,1,0:T(8,128)(2,1)S(1)}, bf16[4,2,4,8,128]{4,3,2,1,0:T(8,128)(2,1)}, u32[]{:S(2)}) copy-start(bf16[4,2,4,8,128]{4,3,2,1,0:T(8,128)(2,1)} %param.26) | copy-start | bytes 196612
  7.2 7.8 %slice-start = ((bf16[2,1024,4,128]{3,2,1,0:T(4,128)(2,1)}), bf16[2,256,4,128]{3,2,1,0:T(4,128)(2,1)S(1)}, s32[]{:S(2)}) async-start(bf16[2,1024,4,128]{3,2,1,0:T(4,128)(2,1)} %param.17), calls=%async_computation.4 | async-start | bytes 1048576 | tf_op jit(solution)/shard_map/slice | solution.py:99
  7.2 12.8 %copy-start.3 = (s32[2]{0:T(128)S(1)}, s32[2]{0:T(128)}, u32[]{:S(2)}) copy-start(s32[2]{0:T(128)} %param.18) | copy-start | bytes 28
  7.2 113.7 %all-gather.8.cloned.1.call-start = ((), (), s32[]{:S(2)}) async-start(), calls=%async_computation | async-start | bytes 6291456 | tf_op jit(solution)/shard_map/all_gather | solution.py:111
  9.2 15.3 %copy-start.4 = (s32[2,16]{1,0:T(2,128)S(1)}, s32[2,16]{1,0:T(2,128)}, u32[]{:S(2)}) copy-start(s32[2,16]{1,0:T(2,128)} %param.19) | copy-start | bytes 388
  9.2 15.3 %copy-start.5 = (s32[2,16]{1,0:T(2,128)S(1)}, s32[2,16]{1,0:T(2,128)}, u32[]{:S(2)}) copy-start(s32[2,16]{1,0:T(2,128)} %param.20) | copy-start | bytes 388
  10.1 32.1 %collective-permute-start = (bf16[2,256,4,128]{3,1,2,0:T(8,128)(2,1)}, bf16[2,256,4,128]{3,1,2,0:T(8,128)(2,1)S(1)}, u32[]{:S(2)}, u32[]{:S(2)}) collective-permute-start(bf16[2,256,4,128]{3,1,2,0:T(8,128)(2,1)} %slice.23), channel_id=1, source_target_pairs={{0,2},{2,4},{4,6},{6,8},{8,10},{10,12},{12,14},{14,16},{16,18},{18... | collective-permute-start | bytes 1572872 | tf_op jit(solution)/shard_map/ppermute | solution.py:21
  15.8 21.8 %collective-permute-start.1 = (bf16[2,256,4,128]{3,1,2,0:T(8,128)(2,1)}, bf16[2,256,4,128]{3,1,2,0:T(8,128)(2,1)}, u32[]{:S(2)}, u32[]{:S(2)}) collective-permute-start(bf16[2,256,4,128]{3,1,2,0:T(8,128)(2,1)} %copy.67), channel_id=1, source_target_pairs={{0,2},{2,4},{4,6},{6,8},{8,10},{10,12},{12,14},{14,16},{16,18},{18... | collective-permute-start | bytes 1572872 | tf_op jit(solution)/shard_map/ppermute | solution.py:21
  100.6 5.8 %copy-start.1 = (bf16[2,256,4,128]{3,2,1,0:T(4,128)(2,1)S(1)}, bf16[2,256,4,128]{3,2,1,0:T(4,128)(2,1)}, u32[]{:S(2)}) copy-start(bf16[2,256,4,128]{3,2,1,0:T(4,128)(2,1)} %param.24) | copy-start | bytes 1572868
  100.6 5.9 %copy-start.2 = (bf16[2,256,4,128]{3,2,1,0:T(4,128)(2,1)S(1)}, bf16[2,256,4,128]{3,2,1,0:T(4,128)(2,1)}, u32[]{:S(2)}) copy-start(bf16[2,256,4,128]{3,2,1,0:T(4,128)(2,1)} %param.25) | copy-start | bytes 1572868
  104.9 132.3 %all-gather.10.cloned.1.call-start = ((), (), s32[]{:S(2)}) async-start(), calls=%async_computation.1 | async-start | bytes 8912896 | tf_op jit(solution)/shard_map/all_gather | solution.py:114
  105.6 244.9 %all-gather.12.cloned.1.call-start = ((), (), s32[]{:S(2)}) async-start(), calls=%async_computation.2 | async-start | bytes 8912896 | tf_op jit(solution)/shard_map/all_gather | solution.py:119
  106.4 335.3 %all-gather.14.cloned.1.call-start = ((), (), s32[]{:S(2)}) async-start(), calls=%async_computation.3 | async-start | bytes 2228224 | tf_op jit(solution)/shard_map/all_gather | solution.py:25
Sparse Core Ops, SparseCore 0:
  105.0 15.8 all-gather.7
  123.7 113.4 all-gather.9
  240.0 110.4 all-gather.11
  361.7 60.6 all-gather.13
where the time goes:
time: 474 us; the launch traced here: 473 us
  waiting for transfers between devices  250 us (53%)
  blocking collectives  81.3 us (17%)
  other arithmetic  51.1 us (11%)
  matrix products  43.6 us (9%)
  local copies, waits for them, and re-layouts  22.9 us (5%)
  between operations  14 us (3%)
  starting transfers between devices  9.39 us (2%)
    all_gather x1, waiting for transfers between devices, body(): lax.all_gather(beacon_wk, 'seq', axis=0, tiled=True)  116 us
    all_gather x1, waiting for transfers between devices, body(): lax.all_gather(beacon_wv, 'seq', axis=0, tiled=True)  106 us
    all_gather x2, blocking collectives, joined(): everything = jax.tree.map(lambda part: lax.all_gather(part, axis), shard)  78 us
    sub x2, other arithmetic, per_request(): weights = jnp.where(cache_mask, jnp.exp(scores - row_peak[..., None]), 0.0)  23.3 us
    add x15, other arithmetic, blend(): former[2] * former_scale[..., None] + latter[2] * latter_scale[..., None]  16.1 us
    dot_general x2, matrix products, per_request(): jnp.einsum('jkgi,ikd->jkgd', weights.astype(jnp.bfloat16), value_block, p...  14.5 us
    all_gather x1, waiting for transfers between devices, body(): pooled_whole = lax.all_gather(pooled_flat, 'head', axis=1, tiled=True)  14.1 us
    ppermute x2, waiting for transfers between devices, shifted(): lax.ppermute(value, axis, [(source, source + steps) for source in range(f...  12.6 us
  transfers between devices with their start and end apart: 6, of which 4 were waited for; matrix products, arithmetic and copies ran while one was open for 4% of the time, Pallas kernels for 0%

commit v1 on v0

--- a/solution.py
+++ b/solution.py
@@ -1,8 +1,11 @@
+import functools
 import math
 
 import jax
 import jax.numpy as jnp
 from jax import lax
+from jax.experimental import pallas as pl
+from jax.experimental.pallas import tpu as pltpu
 from jax.sharding import PartitionSpec as P
 
 G = 8
@@ -162,9 +165,584 @@
     return (beacon_keys, beacon_values, projected)
 
 
+B = 4
+CH = 4
+
+
+def fused_kernel(
+    shard_count,
+    phase_ref,
+    ratio_ref,
+    rlen_ref,
+    k_hbm,
+    v_hbm,
+    q_hbm,
+    wk_hbm,
+    wv_hbm,
+    rk_ref,
+    rv_ref,
+    dq_ref,
+    ow_hbm,
+    bk_ref,
+    bv_ref,
+    proj_ref,
+    kbuf,
+    vbuf,
+    qbuf,
+    wbuf,
+    act,
+    stage,
+    psend,
+    precv,
+    own,
+    bias,
+    owbuf,
+    snd,
+    rcv,
+    att,
+    part,
+    load_sem,
+    rim_send,
+    rim_recv,
+    w_send,
+    w_recv,
+    a_send,
+    a_recv,
+    a_loc,
+    p_send,
+    p_recv,
+    s_send,
+    s_recv,
+    d_send,
+    d_recv,
+    t_send,
+    t_recv,
+    h_send,
+    h_recv,
+):
+    n = shard_count
+    depth = n // B
+    s = lax.axis_index("seq")
+    h = lax.axis_index("head")
+    z = s // B
+    me = lax.rem(s, B)
+    heads, rows, hd = kbuf.shape[1], kbuf.shape[2], kbuf.shape[3]
+    requests = kbuf.shape[0]
+    interval = rows - OFF
+    nb = bias.shape[1]
+    width = wbuf.shape[3]
+    inv_root = 1.0 / math.sqrt(hd)
+    f32 = jnp.float32
+
+    def remote(src, dst, send, recv, seq=None):
+        target = {"head": 1 - h} if seq is None else {"seq": seq}
+        return pltpu.make_async_remote_copy(
+            src_ref=src,
+            dst_ref=dst,
+            send_sem=send,
+            recv_sem=recv,
+            device_id=target,
+            device_id_type=pl.DeviceIdType.MESH,
+        )
+
+    loads = []
+    half = wk_hbm.shape[1] // (CH // 2)
+    for c in range(CH):
+        source = (wk_hbm, wv_hbm)[c // (CH // 2)]
+        first = (c % (CH // 2)) * half
+        loads.append(
+            pltpu.make_async_copy(
+                source.at[:, first : first + half], wbuf.at[z, c], load_sem.at[c]
+            )
+        )
+    loads.append(pltpu.make_async_copy(k_hbm, kbuf.at[:, :, OFF:], load_sem.at[CH]))
+    loads.append(pltpu.make_async_copy(v_hbm, vbuf.at[:, :, OFF:], load_sem.at[CH + 1]))
+    loads.append(pltpu.make_async_copy(q_hbm, qbuf, load_sem.at[CH + 2]))
+    loads.append(pltpu.make_async_copy(ow_hbm, owbuf, load_sem.at[CH + 3]))
+    for copy in loads:
+        copy.start()
+
+    barrier = pltpu.get_barrier_semaphore()
+    for o in range(1, n):
+        pl.semaphore_signal(
+            barrier, inc=1, device_id={"seq": lax.rem(s + o, n)}, device_id_type=pl.DeviceIdType.MESH
+        )
+    pl.semaphore_signal(
+        barrier, inc=1, device_id={"head": 1 - h}, device_id_type=pl.DeviceIdType.MESH
+    )
+    pl.semaphore_wait(barrier, n)
+
+    def rim(which):
+        source, target = ((k_hbm, kbuf), (v_hbm, vbuf))[which]
+        return remote(
+            source.at[:, :, interval - OFF :],
+            target.at[:, :, :OFF],
+            rim_send.at[which],
+            rim_recv.at[which],
+            lax.rem(s + 1, n),
+        )
+
+    @pl.when(s < n - 1)
+    def _():
+        rim(0).start()
+        rim(1).start()
+
+    @pl.when(s == 0)
+    def _():
+        kbuf[:, :, :OFF] = jnp.zeros((requests, heads, OFF, hd), kbuf.dtype)
+        vbuf[:, :, :OFF] = jnp.zeros((requests, heads, OFF, hd), vbuf.dtype)
+
+    def w_copy(way, d, c, shard, target):
+        return remote(
+            wbuf.at[shard, c],
+            wbuf.at[shard, c],
+            w_send.at[way, d, c],
+            w_recv.at[way, d, c],
+            target * B + me,
+        )
+
+    def w_out(way, d):
+        if way == 0:
+            return z - d, z + 1, (z - d >= 0) & (z + 1 < depth)
+        return z + d, z - 1, (z + d < depth) & (z - 1 >= 0)
+
+    def w_in(way, d):
+        if way == 0:
+            return z - 1 - d, z - 1 - d >= 0
+        return z + 1 + d, z + 1 + d < depth
+
+    def w_start(d, c):
+        for way in range(2):
+            shard, target, there = w_out(way, d)
+
+            @pl.when(there)
+            def _(way=way, shard=shard, target=target):
+                w_copy(way, d, c, shard, target).start()
+
+    def w_wait(d, c):
+        for way in range(2):
+            shard, there = w_in(way, d)
+
+            @pl.when(there)
+            def _(way=way, shard=shard):
+                w_copy(way, d, c, shard, z).wait_recv()
+
+    def w_relay(d, c):
+        for way in range(2):
+            shard, there = w_in(way, d - 1)
+            out, target, onward = w_out(way, d)
+
+            @pl.when(there)
+            def _(way=way, shard=shard):
+                w_copy(way, d - 1, c, shard, z).wait_recv()
+
+            @pl.when(onward)
+            def _(way=way, out=out, target=target):
+                w_copy(way, d, c, out, target).start()
+
+    def w_own(c):
+        loads[c].wait()
+        w_start(0, c)
+
+    w_own(0)
+    w_own(1)
+
+    for r in range(requests):
+        slot = lax.broadcasted_iota(jnp.int32, (nb, rows), 0)
+        position = lax.broadcasted_iota(jnp.int32, (nb, rows), 1) - OFF + phase_ref[r]
+        lead = jnp.where(s == 0, phase_ref[r], 0)
+        reach = (slot + 1) * ratio_ref[r, s] + lead
+        allowed = (position >= lead) & (position < interval) & (position < reach)
+        bias[r] = jnp.where(allowed, 0.0, masked_score).astype(f32)
+
+    loads[CH].wait()
+    loads[CH + 1].wait()
+    loads[CH + 2].wait()
+
+    w_relay(1, 0)
+    w_own(2)
+    w_relay(2, 0)
+    w_relay(1, 1)
+    w_own(3)
+
+    @pl.when(s > 0)
+    def _():
+        rim(0).wait_recv()
+        rim(1).wait_recv()
+
+    def a_remote(u, x):
+        kk, r, y = u // 4, lax.rem(u, 2), lax.rem(u // 2, 2)
+        return remote(
+            stage.at[u, x],
+            act.at[h * 2 + kk, me, r],
+            a_send.at[u, x],
+            a_recv.at[kk, r, me],
+            z * B + y * 2 + x,
+        )
+
+    def a_local(kk, r, u):
+        return pltpu.make_async_copy(
+            stage.at[u, lax.rem(me, 2)], act.at[h * 2 + kk, me, r], a_loc.at[kk, r]
+        )
+
+    def a_relay(kk):
+        return remote(
+            act.at[h * 2 + kk], act.at[h * 2 + kk], p_send.at[kk], p_recv.at[kk]
+        )
+
+    def a_gather(kk):
+        for r in range(requests):
+            a_local(kk, r, kk * 4 + (me // 2) * 2 + r).wait()
+            for o in range(1, B):
+                source = lax.rem(me + o, B)
+                remote(
+                    stage.at[0, 0],
+                    act.at[h * 2 + kk, source, r],
+                    a_send.at[0, 0],
+                    a_recv.at[kk, r, source],
+                    s,
+                ).wait_recv()
+        a_relay(kk).start()
+
+    def unit(u, carry):
+        k, r = u // 2, lax.rem(u, 2)
+        for g in range(G):
+            scores = (
+                lax.dot_general(
+                    qbuf[r, k, g],
+                    kbuf[r, k],
+                    (((1,), (1,)), ((), ())),
+                    preferred_element_type=f32,
+                )
+                * inv_root
+                + bias[r]
+            )
+            weights = jnp.exp(scores - jnp.max(scores, axis=-1, keepdims=True))
+            total = jnp.sum(weights, axis=-1, keepdims=True)
+            out = jnp.dot(weights.astype(jnp.bfloat16), vbuf[r, k], preferred_element_type=f32)
+            at = (g % 4) * hd
+            stage[u, g // 4, :, at : at + hd] = (out / total).astype(jnp.bfloat16)
+        for x in range(2):
+            member = lax.rem(k, 2) * 2 + x
+
+            @pl.when(member == me)
+            def _():
+                a_local(u // 4, r, u).start()
+
+            @pl.when(member != me)
+            def _(x=x):
+                a_remote(u, x).start()
+
+        @pl.when(u == 1)
+        def _():
+            w_relay(2, 1)
+            w_relay(1, 2)
+
+        @pl.when(u == 3)
+        def _():
+            w_relay(2, 2)
+
+        @pl.when(u == 5)
+        def _():
+            a_gather(0)
+            w_relay(1, 3)
+
+        return carry
+
+    lax.fori_loop(0, 2 * heads, unit, 0)
+    a_gather(1)
+    w_relay(2, 3)
+    a_relay(0).wait_recv()
+    a_relay(1).wait_recv()
+
+    def p_copy(c, to, frm):
+        return remote(
+            psend.at[to, c], precv.at[frm, c], s_send.at[to, c], s_recv.at[frm, c], z * B + to
+        )
+
+    for c in range(CH):
+        w_wait(depth - 2, c)
+
+        def product(o, carry, c=c):
+            to = lax.rem(me + 1 + o, B)
+            total = jnp.zeros((requests * nb, width), f32)
+            for zi in range(depth):
+                total += jnp.dot(
+                    act[zi, to].reshape(requests * nb, act.shape[4]),
+                    wbuf[zi, c],
+                    preferred_element_type=f32,
+                )
+
+            @pl.when(o < B - 1)
+            def _():
+                psend[to, c] = total.astype(jnp.bfloat16)
+                p_copy(c, to, me).start()
+
+            @pl.when(o == B - 1)
+            def _():
+                own[c] = total
+
+            return carry
+
+        lax.fori_loop(0, B, product, 0)
+
+    slot_row = lax.broadcasted_iota(jnp.int32, (nb, width), 0)
+    for c in range(CH):
+        for o in range(1, B):
+            source = lax.rem(me + o, B)
+            p_copy(c, source, source).wait_recv()
+        total = own[c]
+        for o in range(1, B):
+            total += precv[lax.rem(me + o, B), c].astype(f32)
+        out_ref = (bk_ref, bv_ref)[c // (CH // 2)]
+        at = (c % (CH // 2)) * width
+        for r in range(requests):
+            live = (slot_row + 1) * ratio_ref[r, s] <= interval
+            out_ref[r * nb : (r + 1) * nb, at : at + width] = jnp.where(
+                live, total[r * nb : (r + 1) * nb], 0.0
+            ).astype(jnp.bfloat16)
+
+    res = rk_ref.shape[2]
+    qrows = dq_ref.shape[1]
+    pair = qrows // G
+    cells = res + nb + OFF
+    row_request = lax.rem(lax.broadcasted_iota(jnp.int32, (qrows, cells), 0), pair) // (
+        pair // requests
+    )
+    cell = lax.broadcasted_iota(jnp.int32, (qrows, cells), 1)
+    last = jnp.where(s == n - 1, 1, 0)
+    masks = []
+    for r in range(requests):
+        usable = (
+            (cell < rlen_ref[r, s])
+            | ((cell >= res) & (cell < res + nb) & ((cell - res + 1) * ratio_ref[r, s] <= interval))
+            | ((cell >= res + nb + OFF - phase_ref[r] * last) & (cell >= res + nb))
+        )
+        masks.append(usable & (row_request == r))
+    share = G * heads // n
+    for k in range(heads):
+        lanes = slice(k * hd, (k + 1) * hd)
+        pieces = []
+        for r in range(requests):
+            keys = (rk_ref[r, k], bk_ref[r * nb : (r + 1) * nb, lanes], kbuf[r, k, rows - OFF :])
+            scores = jnp.concatenate(
+                [
+                    lax.dot_general(
+                        dq_ref[k], key, (((1,), (1,)), ((), ())), preferred_element_type=f32
+                    )
+                    for key in keys
+                ],
+                axis=1,
+            )
+            pieces.append(jnp.where(masks[r], scores * inv_root, masked_score))
+        peak = jnp.maximum(
+            jnp.max(pieces[0], axis=-1, keepdims=True), jnp.max(pieces[1], axis=-1, keepdims=True)
+        )
+        total = jnp.zeros((qrows, 1), f32)
+        out = jnp.zeros((qrows, hd), f32)
+        for r in range(requests):
+            weights = jnp.exp(pieces[r] - peak)
+            total += jnp.sum(weights, axis=-1, keepdims=True)
+            low = weights.astype(jnp.bfloat16)
+            out += jnp.dot(low[:, :res], rv_ref[r, k], preferred_element_type=f32)
+            out += jnp.dot(
+                low[:, res : res + nb],
+                bv_ref[r * nb : (r + 1) * nb, lanes],
+                preferred_element_type=f32,
+            )
+            out += jnp.dot(
+                low[:, res + nb :], vbuf[r, k, rows - OFF :], preferred_element_type=f32
+            )
+        lane = lax.broadcasted_iota(jnp.int32, (qrows, hd), 1)
+        stats = jnp.where(lane < hd // 2, peak, total)
+        snd[k * G : (k + 1) * G, 0] = out.reshape(G, pair, hd)
+        snd[k * G : (k + 1) * G, 1] = stats.reshape(G, pair, hd)
+
+    def d_copy(to, frm):
+        return remote(
+            snd.at[pl.ds(to * share, share)], rcv.at[frm], d_send.at[to], d_recv.at[frm], to
+        )
+
+    def t_copy(to, frm):
+        return remote(att.at[frm], att.at[frm], t_send.at[to], t_recv.at[frm], to)
+
+    for o in range(1, n):
+        d_copy(lax.rem(s + o, n), s).start()
+    rcv[s] = snd[pl.ds(s * share, share)]
+    for o in range(1, n):
+        source = lax.rem(s + o, n)
+        d_copy(source, source).wait_recv()
+    peaks = rcv[:, :, 1, :, 0:1]
+    sums = rcv[:, :, 1, :, hd // 2 : hd // 2 + 1]
+    scale = jnp.exp(peaks - jnp.max(peaks, axis=0, keepdims=True))
+    att[s] = jnp.sum(scale * rcv[:, :, 0], axis=0) / jnp.sum(scale * sums, axis=0)
+    for o in range(1, n):
+        t_copy(lax.rem(s + o, n), s).start()
+    for o in range(1, n):
+        source = lax.rem(s + o, n)
+        t_copy(source, source).wait_recv()
+    loads[CH + 3].wait()
+    vectors = jnp.concatenate(
+        [att[i, j].astype(jnp.bfloat16) for i in range(n) for j in range(share)], axis=1
+    )
+    partial_value = jnp.dot(vectors, owbuf[...], preferred_element_type=f32)
+    part[0] = partial_value
+    swap = remote(part.at[0], part.at[1], h_send, h_recv)
+    swap.start()
+    swap.wait_recv()
+    first = jnp.where(h == 0, part[0], part[1])
+    second = jnp.where(h == 0, part[1], part[0])
+    proj_ref[...] = (first + second).astype(jnp.bfloat16)
+
+    swap.wait_send()
+    for o in range(1, n):
+        d_copy(lax.rem(s + o, n), s).wait_send()
+        t_copy(lax.rem(s + o, n), s).wait_send()
+    for c in range(CH):
+        for o in range(1, B):
+            p_copy(c, lax.rem(me + o, B), me).wait_send()
+    a_relay(0).wait_send()
+    a_relay(1).wait_send()
+    for u in range(2 * heads):
+        for x in range(2):
+
+            @pl.when((u // 2 % 2) * 2 + x != me)
+            def _(u=u, x=x):
+                a_remote(jnp.int32(u), x).wait_send()
+
+    for way in range(2):
+        for d in range(depth - 1):
+            shard, target, there = w_out(way, d)
+            for c in range(CH):
+
+                @pl.when(there)
+                def _(way=way, d=d, c=c, shard=shard, target=target):
+                    w_copy(way, d, c, shard, target).wait_send()
+
+    @pl.when(s < n - 1)
+    def _():
+        rim(0).wait_send()
+        rim(1).wait_send()
+
+
+def fused_body(
+    shard_count,
+    raw_keys,
+    raw_values,
+    phase,
+    ratio,
+    resident_len,
+    beacon_queries,
+    beacon_wk,
+    beacon_wv,
+    resident_keys,
+    resident_values,
+    decode_queries,
+    out_weight,
+):
+    n = shard_count
+    depth = n // B
+    requests, interval, heads, hd = raw_keys.shape
+    steps = decode_queries.shape[0]
+    nb = beacon_queries.shape[1]
+    rows = interval + OFF
+    by_head = (0, 2, 1, 3)
+    feature, columns = beacon_wk.shape
+    width = 2 * columns // CH
+    pair = requests * steps
+    share = G * heads // n
+    bf16, f32 = jnp.bfloat16, jnp.float32
+    dma = pltpu.SemaphoreType.DMA
+    smem = pl.BlockSpec(memory_space=pltpu.SMEM)
+    anywhere = pl.BlockSpec(memory_space=pl.ANY)
+    vmem = pl.BlockSpec(memory_space=pltpu.VMEM)
+    keys, values, projected = pl.pallas_call(
+        functools.partial(fused_kernel, n),
+        out_shape=(
+            jax.ShapeDtypeStruct((requests * nb, columns), bf16),
+            jax.ShapeDtypeStruct((requests * nb, columns), bf16),
+            jax.ShapeDtypeStruct((pair, out_weight.shape[1]), bf16),
+        ),
+        in_specs=[smem] * 3 + [anywhere] * 5 + [vmem] * 3 + [anywhere],
+        out_specs=(vmem, vmem, vmem),
+        scratch_shapes=[
+            pltpu.VMEM((requests, heads, rows, hd), bf16),
+            pltpu.VMEM((requests, heads, rows, hd), bf16),
+            pltpu.VMEM((requests, heads, G, nb, hd), bf16),
+            pltpu.VMEM((depth, CH, feature, width), bf16),
+            pltpu.VMEM((depth, B, requests, nb, feature), bf16),
+            pltpu.VMEM((requests * heads, 2, nb, feature), bf16),
+            pltpu.VMEM((B, CH, requests * nb, width), bf16),
+            pltpu.VMEM((B, CH, requests * nb, width), bf16),
+            pltpu.VMEM((CH, requests * nb, width), f32),
+            pltpu.VMEM((requests, nb, rows), f32),
+            pltpu.VMEM(out_weight.shape, bf16),
+            pltpu.VMEM((G * heads, 2, pair, hd), f32),
+            pltpu.VMEM((n, share, 2, pair, hd), f32),
+            pltpu.VMEM((n, share, pair, hd), f32),
+            pltpu.VMEM((2, pair, out_weight.shape[1]), f32),
+            dma((CH + 4,)),
+            dma((2,)),
+            dma((2,)),
+            dma((2, depth - 1, CH)),
+            dma((2, depth - 1, CH)),
+            dma((requests * heads, 2)),
+            dma((2, requests, B)),
+            dma((2, requests)),
+            dma((2,)),
+            dma((2,)),
+            dma((B, CH)),
+            dma((B, CH)),
+            dma((n,)),
+            dma((n,)),
+            dma((n,)),
+            dma((n,)),
+            dma,
+            dma,
+        ],
+        compiler_params=pltpu.CompilerParams(
+            collective_id=0, has_side_effects=True, vmem_limit_bytes=60 * 1024 * 1024
+        ),
+    )(
+        phase,
+        ratio,
+        resident_len,
+        jnp.transpose(raw_keys, by_head),
+        jnp.transpose(raw_values, by_head),
+        jnp.transpose(beacon_queries, (0, 2, 3, 1, 4)),
+        beacon_wk,
+        beacon_wv,
+        jnp.transpose(resident_keys, by_head),
+        jnp.transpose(resident_values, by_head),
+        jnp.transpose(decode_queries, (2, 3, 1, 0, 4)).reshape(heads, G * pair, hd),
+        out_weight,
+    )
+    return (
+        keys.reshape(requests, nb, heads, hd),
+        values.reshape(requests, nb, heads, hd),
+        jnp.transpose(projected.reshape(requests, steps, -1), (1, 0, 2)),
+    )
+
+
+def chosen_body(shard_count, head_count):
+    def run(*arrays):
+        requests, _, heads, hd = arrays[0].shape
+        feature = arrays[6].shape[0]
+        fits = (
+            head_count == 2
+            and shard_count == B * B
+            and requests == 2
+            and heads == B
+            and 2 * feature == G * hd
+        )
+        return fused_body(shard_count, *arrays) if fits else body(*arrays)
+
+    return run
+
+
 def solution(mesh):
     return jax.shard_map(
-        body,
+        chosen_body(mesh.shape["seq"], mesh.shape["head"]),
         mesh=mesh,
         in_specs=(
             P(None, "seq", "head", None),

time: 474 us -> 158 us (0.33)
  waiting for transfers between devices: 250 us -> 0 us
  Pallas kernels: 0 us -> 143 us
  blocking collectives: 81.3 us -> 0 us
  other arithmetic: 51.1 us -> 0 us
  matrix products: 43.6 us -> 0 us
  between operations: 14 us -> 0.66 us
  starting transfers between devices: 9.39 us -> 0 us
  local copies, waits for them, and re-layouts: 22.9 us -> 14.5 us
    all_gather x4 -> x0, waiting for transfers between devices: 237 us -> none  [the longest x1 116 us: body(): lax.all_gather(beacon_wk, 'seq', axis=0, tiled=True)]
    pallas_call x0 -> x1, Pallas kernels: none -> 143 us  [fused_body(): pl.pallas_call(functools.partial(fused_kernel, n), out_shape=(jax.ShapeDt...]
    all_gather x2 -> x0, blocking collectives: 78 us -> none  [joined(): everything = jax.tree.map(lambda part: lax.all_gather(part, axis), shard)]
    dot_general x9 -> x0, matrix products: 43.6 us -> none  [the longest x2 14.5 us: per_request(): jnp.einsum('jkgi,ikd->jkgd', weights.astype(jnp.bfloat16), value_block, p...]
    sub x4 -> x0, other arithmetic: 23.3 us -> none  [the longest x2 23.3 us: per_request(): weights = jnp.where(cache_mask, jnp.exp(scores - row_peak[..., None]), 0.0)]
    add x34 -> x0, other arithmetic: 16.9 us -> none  [the longest x15 16.1 us: blend(): former[2] * former_scale[..., None] + latter[2] * latter_scale[..., None]]
    ppermute x2 -> x0, waiting for transfers between devices: 12.6 us -> none  [shifted(): lax.ppermute(value, axis, [(source, source + steps) for source in range(f...]
    ppermute x2 -> x0, starting transfers between devices: 9.05 us -> none  [shifted(): lax.ppermute(value, axis, [(source, source + steps) for source in range(f...]
  transfers between devices with their start and end apart: 6 -> 0, of which waited for: 4 -> 0; matrix products, arithmetic and copies ran while one was open for 4% -> 0% of each run, Pallas kernels for 0% -> 0%
where the time goes in v1:
time: 158 us
  Pallas kernels  143 us (91%)
  local copies, waits for them, and re-layouts  14.5 us (9%)
    pallas_call x1, Pallas kernels, fused_body(): pl.pallas_call(functools.partial(fused_kernel, n), out_shape=(jax.ShapeDt...  143 us

profile of v1, /device:TPU:0, one launch (start us, length us, event | category | flops | bytes accessed | tf_op | source)
XLA Modules:
  0.0 157.7 jit_solution(17520961865438986813)
XLA Ops:
  0.6 0.0 copy-start
  0.6 1.7 %copy.20 = bf16[4,8,2,4,128]{4,3,2,1,0:T(4,128)(2,1)} copy(bf16[4,8,2,4,128]{4,1,0,2,3:T(8,128)(2,1)} %bitcast.18) | data formatting | bytes 131072 | tf_op jit(solution)/shard_map/transpose | solution.py:717
  2.3 2.4 %copy_bitcast_fusion.3 = (bf16[2,4,256,128]{3,2,1,0:T(8,128)(2,1)}, bf16[2,4,256,128]{3,2,1,0:T(8,128)(2,1)}) fusion(bf16[2,256,4,128]{3,2,1,0:T(4,128)(2,1)} %param.21, bf16[2,256,4,128]{3,2,1,0:T(4,128)(2,1)} %param.20), kind=kLoop, calls=%fused_computation.3 | loop fusion | bytes 2097152 | tf_op jit(solution)/shard_map/transpose | solution.py:716
  4.7 0.0 copy-done
  4.7 0.0 copy-start.1
  4.7 0.0 copy-start.2
  4.7 2.1 %copy.28 = bf16[2,128,4,8,128]{4,1,3,2,0:T(8,128)(2,1)} copy(bf16[2,128,4,8,128]{4,3,2,1,0:T(8,128)(2,1)S(1)} %copy-done) | data formatting | bytes 4194304 | tf_op args[5]
  6.9 0.0 copy-done.1
  6.9 0.8 copy-done.2
  7.7 2.7 %copy_bitcast_fusion.1 = (bf16[2,4,1024,128]{3,2,1,0:T(8,128)(2,1)}, bf16[2,4,1024,128]{3,2,1,0:T(8,128)(2,1)}) fusion(bf16[2,1024,4,128]{3,2,1,0:T(4,128)(2,1)S(1)} %copy-done.1, bf16[2,1024,4,128]{3,2,1,0:T(4,128)(2,1)S(1)} %copy-done.2), kind=kLoop, calls=%fused_computation.1 | loop fusion | bytes 8388608 | tf_op jit(solution)/shard_map/transpose | solution.py:711
  10.4 142.6 %shard_map.139 = (bf16[256,512]{1,0:T(8,128)(2,1)}, bf16[256,512]{1,0:T(8,128)(2,1)}, bf16[8,512]{1,0:T(8,128)(2,1)}) custom-call(s32[2]{0:T(128)} %phase_ref.1, s32[2,16]{1,0:T(2,128)} %ratio_ref.1, s32[2,16]{1,0:T(2,128)} %rlen_ref.1, bf16[2,4,1024,128]{3,2,1,0:T(8,128)(2,1)} %get-tuple-element.10.k_hbm, bf16[2,4,1024,128]{3,2,1,0:T(8,128)(2,1)} %get-tuple-element.9.v_hbm, ...), custom_call_target="tpu_custom_call" | custom-call | tf_op jit(solution)/shard_map/pallas_call | solution.py:659
  153.0 1.7 %reshape.19 = bf16[2,128,4,128]{3,2,1,0:T(4,128)(2,1)} reshape(bf16[256,512]{1,0:T(8,128)(2,1)} %get-tuple-element.6) | data formatting | bytes 524288 | tf_op jit(solution)/shard_map/reshape | solution.py:721
  154.7 0.7 reshape.21
  155.4 0.6 copy.29
  156.0 1.7 %reshape.20 = bf16[2,128,4,128]{3,2,1,0:T(4,128)(2,1)} reshape(bf16[256,512]{1,0:T(8,128)(2,1)} %get-tuple-element.7) | data formatting | bytes 524288 | tf_op jit(solution)/shard_map/reshape | solution.py:722
Async XLA Ops:
  0.6 4.1 %copy-start = (bf16[2,128,4,8,128]{4,3,2,1,0:T(8,128)(2,1)S(1)}, bf16[2,128,4,8,128]{4,3,2,1,0:T(8,128)(2,1)}, u32[]{:S(2)}) copy-start(bf16[2,128,4,8,128]{4,3,2,1,0:T(8,128)(2,1)} %param.17) | copy-start | bytes 6291460
  4.7 2.1 %copy-start.1 = (bf16[2,1024,4,128]{3,2,1,0:T(4,128)(2,1)S(1)}, bf16[2,1024,4,128]{3,2,1,0:T(4,128)(2,1)}, u32[]{:S(2)}) copy-start(bf16[2,1024,4,128]{3,2,1,0:T(4,128)(2,1)} %param.13) | copy-start | bytes 6291460
  4.7 3.0 %copy-start.2 = (bf16[2,1024,4,128]{3,2,1,0:T(4,128)(2,1)S(1)}, bf16[2,1024,4,128]{3,2,1,0:T(4,128)(2,1)}, u32[]{:S(2)}) copy-start(bf16[2,1024,4,128]{3,2,1,0:T(4,128)(2,1)} %param.12) | copy-start | bytes 6291460

commit v2 on v1

--- a/solution.py
+++ b/solution.py
@@ -198,7 +198,9 @@
     bias,
     owbuf,
     snd,
+    snd_stats,
     rcv,
+    rcv_stats,
     att,
     part,
     load_sem,
@@ -215,6 +217,8 @@
     s_recv,
     d_send,
     d_recv,
+    e_send,
+    e_recv,
     t_send,
     t_recv,
     h_send,
@@ -272,20 +276,21 @@
     )
     pl.semaphore_wait(barrier, n)
 
-    def rim(which):
+    def rim(which, k):
         source, target = ((k_hbm, kbuf), (v_hbm, vbuf))[which]
         return remote(
-            source.at[:, :, interval - OFF :],
-            target.at[:, :, :OFF],
-            rim_send.at[which],
-            rim_recv.at[which],
+            source.at[:, k, interval - OFF :],
+            target.at[:, k, :OFF],
+            rim_send.at[which, k],
+            rim_recv.at[which, k],
             lax.rem(s + 1, n),
         )
 
     @pl.when(s < n - 1)
     def _():
-        rim(0).start()
-        rim(1).start()
+        for k in range(heads):
+            rim(0, k).start()
+            rim(1, k).start()
 
     @pl.when(s == 0)
     def _():
@@ -344,8 +349,8 @@
         loads[c].wait()
         w_start(0, c)
 
-    w_own(0)
-    w_own(1)
+    for c in range(CH):
+        w_own(c)
 
     for r in range(requests):
         slot = lax.broadcasted_iota(jnp.int32, (nb, rows), 0)
@@ -358,17 +363,6 @@
     loads[CH].wait()
     loads[CH + 1].wait()
     loads[CH + 2].wait()
-
-    w_relay(1, 0)
-    w_own(2)
-    w_relay(2, 0)
-    w_relay(1, 1)
-    w_own(3)
-
-    @pl.when(s > 0)
-    def _():
-        rim(0).wait_recv()
-        rim(1).wait_recv()
 
     def a_remote(u, x):
         kk, r, y = u // 4, lax.rem(u, 2), lax.rem(u // 2, 2)
@@ -406,6 +400,12 @@
 
     def unit(u, carry):
         k, r = u // 2, lax.rem(u, 2)
+
+        @pl.when((r == 0) & (s > 0))
+        def _():
+            rim(0, k).wait_recv()
+            rim(1, k).wait_recv()
+
         for g in range(G):
             scores = (
                 lax.dot_general(
@@ -433,25 +433,22 @@
             def _(x=x):
                 a_remote(u, x).start()
 
-        @pl.when(u == 1)
-        def _():
-            w_relay(2, 1)
-            w_relay(1, 2)
-
         @pl.when(u == 3)
         def _():
-            w_relay(2, 2)
-
-        @pl.when(u == 5)
+            w_relay(1, 0)
+
+        @pl.when(u == 6)
         def _():
             a_gather(0)
-            w_relay(1, 3)
 
         return carry
 
     lax.fori_loop(0, 2 * heads, unit, 0)
+    w_relay(2, 0)
+    w_relay(1, 1)
     a_gather(1)
-    w_relay(2, 3)
+    w_relay(2, 1)
+    w_relay(1, 2)
     a_relay(0).wait_recv()
     a_relay(1).wait_recv()
 
@@ -460,34 +457,9 @@
             psend.at[to, c], precv.at[frm, c], s_send.at[to, c], s_recv.at[frm, c], z * B + to
         )
 
-    for c in range(CH):
-        w_wait(depth - 2, c)
-
-        def product(o, carry, c=c):
-            to = lax.rem(me + 1 + o, B)
-            total = jnp.zeros((requests * nb, width), f32)
-            for zi in range(depth):
-                total += jnp.dot(
-                    act[zi, to].reshape(requests * nb, act.shape[4]),
-                    wbuf[zi, c],
-                    preferred_element_type=f32,
-                )
-
-            @pl.when(o < B - 1)
-            def _():
-                psend[to, c] = total.astype(jnp.bfloat16)
-                p_copy(c, to, me).start()
-
-            @pl.when(o == B - 1)
-            def _():
-                own[c] = total
-
-            return carry
-
-        lax.fori_loop(0, B, product, 0)
-
     slot_row = lax.broadcasted_iota(jnp.int32, (nb, width), 0)
-    for c in range(CH):
+
+    def finish(c):
         for o in range(1, B):
             source = lax.rem(me + o, B)
             p_copy(c, source, source).wait_recv()
@@ -501,6 +473,40 @@
             out_ref[r * nb : (r + 1) * nb, at : at + width] = jnp.where(
                 live, total[r * nb : (r + 1) * nb], 0.0
             ).astype(jnp.bfloat16)
+
+    for c in range(CH):
+        if c == 1:
+            w_relay(2, 2)
+            w_relay(1, 3)
+        if c == 2:
+            w_relay(2, 3)
+        w_wait(depth - 2, c)
+
+        def product(o, carry, c=c):
+            to = lax.rem(me + 1 + o, B)
+            total = jnp.zeros((requests * nb, width), f32)
+            for zi in range(depth):
+                total += jnp.dot(
+                    act[zi, to].reshape(requests * nb, act.shape[4]),
+                    wbuf[zi, c],
+                    preferred_element_type=f32,
+                )
+
+            @pl.when(o < B - 1)
+            def _():
+                psend[to, c] = total.astype(jnp.bfloat16)
+                p_copy(c, to, me).start()
+
+            @pl.when(o == B - 1)
+            def _():
+                own[c] = total
+
+            return carry
+
+        lax.fori_loop(0, B, product, 0)
+        if c > 0:
+            finish(c - 1)
+    finish(CH - 1)
 
     res = rk_ref.shape[2]
     qrows = dq_ref.shape[1]
@@ -554,37 +560,55 @@
                 low[:, res + nb :], vbuf[r, k, rows - OFF :], preferred_element_type=f32
             )
         lane = lax.broadcasted_iota(jnp.int32, (qrows, hd), 1)
-        stats = jnp.where(lane < hd // 2, peak, total)
-        snd[k * G : (k + 1) * G, 0] = out.reshape(G, pair, hd)
-        snd[k * G : (k + 1) * G, 1] = stats.reshape(G, pair, hd)
+        slots = hd // (2 * share)
+        stats = jnp.where(lax.rem(lane // slots, 2) == 0, peak, total)
+        stats = stats.reshape(G // share, share, pair, hd)
+        lane = lax.broadcasted_iota(jnp.int32, (G // share, pair, hd), 2)
+        packed = stats[:, 0]
+        for j in range(1, share):
+            packed = jnp.where(lane >= 2 * slots * j, stats[:, j], packed)
+        dests = slice(k * G // share, (k + 1) * G // share)
+        snd[dests] = out.reshape(G // share, share * pair, hd).astype(jnp.bfloat16)
+        snd_stats[dests] = packed
 
     def d_copy(to, frm):
-        return remote(
-            snd.at[pl.ds(to * share, share)], rcv.at[frm], d_send.at[to], d_recv.at[frm], to
-        )
+        return remote(snd.at[to], rcv.at[frm], d_send.at[to], d_recv.at[frm], to)
+
+    def e_copy(to, frm):
+        return remote(snd_stats.at[to], rcv_stats.at[frm], e_send.at[to], e_recv.at[frm], to)
 
     def t_copy(to, frm):
         return remote(att.at[frm], att.at[frm], t_send.at[to], t_recv.at[frm], to)
 
     for o in range(1, n):
+        e_copy(lax.rem(s + o, n), s).start()
         d_copy(lax.rem(s + o, n), s).start()
-    rcv[s] = snd[pl.ds(s * share, share)]
+    rcv[s] = snd[s]
+    rcv_stats[s] = snd_stats[s]
     for o in range(1, n):
         source = lax.rem(s + o, n)
+        e_copy(source, source).wait_recv()
         d_copy(source, source).wait_recv()
-    peaks = rcv[:, :, 1, :, 0:1]
-    sums = rcv[:, :, 1, :, hd // 2 : hd // 2 + 1]
-    scale = jnp.exp(peaks - jnp.max(peaks, axis=0, keepdims=True))
-    att[s] = jnp.sum(scale * rcv[:, :, 0], axis=0) / jnp.sum(scale * sums, axis=0)
+    landed = rcv[...].astype(f32)
+    attended = []
+    for j in range(share):
+        at = 2 * slots * j
+        peaks = rcv_stats[:, :, at : at + 1]
+        sums = rcv_stats[:, :, at + slots : at + slots + 1]
+        scale = jnp.exp(peaks - jnp.max(peaks, axis=0, keepdims=True))
+        mixed = jnp.sum(scale * landed[:, j * pair : (j + 1) * pair], axis=0)
+        attended.append(mixed / jnp.sum(scale * sums, axis=0))
+    att[s] = jnp.concatenate(attended, axis=0).astype(jnp.bfloat16)
     for o in range(1, n):
         t_copy(lax.rem(s + o, n), s).start()
     for o in range(1, n):
         source = lax.rem(s + o, n)
         t_copy(source, source).wait_recv()
     loads[CH + 3].wait()
+    wide = [att[i].astype(f32) for i in range(n)]
     vectors = jnp.concatenate(
-        [att[i, j].astype(jnp.bfloat16) for i in range(n) for j in range(share)], axis=1
-    )
+        [wide[i][j * pair : (j + 1) * pair] for i in range(n) for j in range(share)], axis=1
+    ).astype(jnp.bfloat16)
     partial_value = jnp.dot(vectors, owbuf[...], preferred_element_type=f32)
     part[0] = partial_value
     swap = remote(part.at[0], part.at[1], h_send, h_recv)
@@ -597,6 +621,7 @@
     swap.wait_send()
     for o in range(1, n):
         d_copy(lax.rem(s + o, n), s).wait_send()
+        e_copy(lax.rem(s + o, n), s).wait_send()
         t_copy(lax.rem(s + o, n), s).wait_send()
     for c in range(CH):
         for o in range(1, B):
@@ -621,8 +646,9 @@
 
     @pl.when(s < n - 1)
     def _():
-        rim(0).wait_send()
-        rim(1).wait_send()
+        for k in range(heads):
+            rim(0, k).wait_send()
+            rim(1, k).wait_send()
 
 
 def fused_body(
@@ -677,13 +703,15 @@
             pltpu.VMEM((CH, requests * nb, width), f32),
             pltpu.VMEM((requests, nb, rows), f32),
             pltpu.VMEM(out_weight.shape, bf16),
-            pltpu.VMEM((G * heads, 2, pair, hd), f32),
-            pltpu.VMEM((n, share, 2, pair, hd), f32),
-            pltpu.VMEM((n, share, pair, hd), f32),
+            pltpu.VMEM((n, share * pair, hd), bf16),
+            pltpu.VMEM((n, pair, hd), f32),
+            pltpu.VMEM((n, share * pair, hd), bf16),
+            pltpu.VMEM((n, pair, hd), f32),
+            pltpu.VMEM((n, share * pair, hd), bf16),
             pltpu.VMEM((2, pair, out_weight.shape[1]), f32),
             dma((CH + 4,)),
-            dma((2,)),
-            dma((2,)),
+            dma((2, heads)),
+            dma((2, heads)),
             dma((2, depth - 1, CH)),
             dma((2, depth - 1, CH)),
             dma((requests * heads, 2)),
@@ -693,6 +721,8 @@
             dma((2,)),
             dma((B, CH)),
             dma((B, CH)),
+            dma((n,)),
+            dma((n,)),
             dma((n,)),
             dma((n,)),
             dma((n,)),

time: 158 us -> 139 us (0.88)
  Pallas kernels: 143 us -> 123 us
    pallas_call x1, Pallas kernels: 143 us -> 123 us  [fused_body(): pl.pallas_call(functools.partial(fused_kernel, n), out_shape=(jax.ShapeDt...]
where the time goes in v2:
time: 139 us; the launch traced here: 138 us
  Pallas kernels  123 us (88%)
  local copies, waits for them, and re-layouts  14.5 us (10%)
    pallas_call x1, Pallas kernels, fused_body(): pl.pallas_call(functools.partial(fused_kernel, n), out_shape=(jax.ShapeDt...  123 us
    unnamed x7, local copies, waits for them, and re-layouts  2.98 us

profile of v2, /device:TPU:0, one launch (start us, length us, event | category | flops | bytes accessed | tf_op | source)
XLA Modules:
  0.0 138.4 jit_solution(13185511196889625624)
XLA Ops:
  0.6 0.0 copy-start
  0.6 1.7 %copy.20 = bf16[4,8,2,4,128]{4,3,2,1,0:T(4,128)(2,1)} copy(bf16[4,8,2,4,128]{4,1,0,2,3:T(8,128)(2,1)} %bitcast.18) | data formatting | bytes 131072 | tf_op jit(solution)/shard_map/transpose | solution.py:747
  2.3 2.4 %copy_bitcast_fusion.3 = (bf16[2,4,256,128]{3,2,1,0:T(8,128)(2,1)}, bf16[2,4,256,128]{3,2,1,0:T(8,128)(2,1)}) fusion(bf16[2,256,4,128]{3,2,1,0:T(4,128)(2,1)} %param.21, bf16[2,256,4,128]{3,2,1,0:T(4,128)(2,1)} %param.20), kind=kLoop, calls=%fused_computation.3 | loop fusion | bytes 2097152 | tf_op jit(solution)/shard_map/transpose | solution.py:746
  4.7 0.0 copy-done
  4.7 0.0 copy-start.1
  4.7 0.0 copy-start.2
  4.7 2.1 %copy.28 = bf16[2,128,4,8,128]{4,1,3,2,0:T(8,128)(2,1)} copy(bf16[2,128,4,8,128]{4,3,2,1,0:T(8,128)(2,1)S(1)} %copy-done) | data formatting | bytes 4194304 | tf_op args[5]
  6.9 0.0 copy-done.1
  6.9 0.8 copy-done.2
  7.7 2.7 %copy_bitcast_fusion.1 = (bf16[2,4,1024,128]{3,2,1,0:T(8,128)(2,1)}, bf16[2,4,1024,128]{3,2,1,0:T(8,128)(2,1)}) fusion(bf16[2,1024,4,128]{3,2,1,0:T(4,128)(2,1)S(1)} %copy-done.1, bf16[2,1024,4,128]{3,2,1,0:T(4,128)(2,1)S(1)} %copy-done.2), kind=kLoop, calls=%fused_computation.1 | loop fusion | bytes 8388608 | tf_op jit(solution)/shard_map/transpose | solution.py:741
  10.4 123.3 %shard_map.139 = (bf16[256,512]{1,0:T(8,128)(2,1)}, bf16[256,512]{1,0:T(8,128)(2,1)}, bf16[8,512]{1,0:T(8,128)(2,1)}) custom-call(s32[2]{0:T(128)} %phase_ref.1, s32[2,16]{1,0:T(2,128)} %ratio_ref.1, s32[2,16]{1,0:T(2,128)} %rlen_ref.1, bf16[2,4,1024,128]{3,2,1,0:T(8,128)(2,1)} %get-tuple-element.10.k_hbm, bf16[2,4,1024,128]{3,2,1,0:T(8,128)(2,1)} %get-tuple-element.9.v_hbm, ...), custom_call_target="tpu_custom_call" | custom-call | tf_op jit(solution)/shard_map/pallas_call | solution.py:685
  133.7 1.7 %reshape.19 = bf16[2,128,4,128]{3,2,1,0:T(4,128)(2,1)} reshape(bf16[256,512]{1,0:T(8,128)(2,1)} %get-tuple-element.6) | data formatting | bytes 524288 | tf_op jit(solution)/shard_map/reshape | solution.py:751
  135.4 0.7 reshape.21
  136.1 0.6 copy.29
  136.7 1.7 %reshape.20 = bf16[2,128,4,128]{3,2,1,0:T(4,128)(2,1)} reshape(bf16[256,512]{1,0:T(8,128)(2,1)} %get-tuple-element.7) | data formatting | bytes 524288 | tf_op jit(solution)/shard_map/reshape | solution.py:752
Async XLA Ops:
  0.6 4.1 %copy-start = (bf16[2,128,4,8,128]{4,3,2,1,0:T(8,128)(2,1)S(1)}, bf16[2,128,4,8,128]{4,3,2,1,0:T(8,128)(2,1)}, u32[]{:S(2)}) copy-start(bf16[2,128,4,8,128]{4,3,2,1,0:T(8,128)(2,1)} %param.17) | copy-start | bytes 6291460
  4.7 2.1 %copy-start.1 = (bf16[2,1024,4,128]{3,2,1,0:T(4,128)(2,1)S(1)}, bf16[2,1024,4,128]{3,2,1,0:T(4,128)(2,1)}, u32[]{:S(2)}) copy-start(bf16[2,1024,4,128]{3,2,1,0:T(4,128)(2,1)} %param.13) | copy-start | bytes 6291460
  4.7 3.0 %copy-start.2 = (bf16[2,1024,4,128]{3,2,1,0:T(4,128)(2,1)S(1)}, bf16[2,1024,4,128]{3,2,1,0:T(4,128)(2,1)}, u32[]{:S(2)}) copy-start(bf16[2,1024,4,128]{3,2,1,0:T(4,128)(2,1)} %param.12) | copy-start | bytes 6291460

commit v3 on v2

--- a/solution.py
+++ b/solution.py
@@ -179,8 +179,8 @@
     q_hbm,
     wk_hbm,
     wv_hbm,
-    rk_ref,
-    rv_ref,
+    rk_raw,
+    rv_raw,
     dq_ref,
     ow_hbm,
     bk_ref,
@@ -197,6 +197,8 @@
     own,
     bias,
     owbuf,
+    rk_ref,
+    rv_ref,
     snd,
     snd_stats,
     rcv,
@@ -446,6 +448,9 @@
     lax.fori_loop(0, 2 * heads, unit, 0)
     w_relay(2, 0)
     w_relay(1, 1)
+    for r in range(requests):
+        rk_ref[r] = jnp.swapaxes(rk_raw[r], 0, 1)
+        rv_ref[r] = jnp.swapaxes(rv_raw[r], 0, 1)
     a_gather(1)
     w_relay(2, 1)
     w_relay(1, 2)
@@ -703,6 +708,8 @@
             pltpu.VMEM((CH, requests * nb, width), f32),
             pltpu.VMEM((requests, nb, rows), f32),
             pltpu.VMEM(out_weight.shape, bf16),
+            pltpu.VMEM((requests, heads, resident_keys.shape[1], hd), bf16),
+            pltpu.VMEM((requests, heads, resident_keys.shape[1], hd), bf16),
             pltpu.VMEM((n, share * pair, hd), bf16),
             pltpu.VMEM((n, pair, hd), f32),
             pltpu.VMEM((n, share * pair, hd), bf16),
@@ -742,8 +749,8 @@
         jnp.transpose(beacon_queries, (0, 2, 3, 1, 4)),
         beacon_wk,
         beacon_wv,
-        jnp.transpose(resident_keys, by_head),
-        jnp.transpose(resident_values, by_head),
+        resident_keys,
+        resident_values,
         jnp.transpose(decode_queries, (2, 3, 1, 0, 4)).reshape(heads, G * pair, hd),
         out_weight,
     )

time: 139 us -> 137 us (0.986)
  local copies, waits for them, and re-layouts: 14.5 us -> 12.8 us
    transpose x1 -> x0, local copies, waits for them, and re-layouts: 2.42 us -> none  [fused_body(): jnp.transpose(resident_values, by_head)]
    unnamed x7 -> x5, local copies, waits for them, and re-layouts: 2.98 us -> 3.88 us
where the time goes in v3:
time: 137 us
  Pallas kernels  123 us (90%)
  local copies, waits for them, and re-layouts  12.8 us (9%)
    pallas_call x1, Pallas kernels, fused_body(): pl.pallas_call(functools.partial(fused_kernel, n), out_shape=(jax.ShapeDt...  123 us
    unnamed x5, local copies, waits for them, and re-layouts  3.88 us

profile of v3, /device:TPU:0, one launch (start us, length us, event | category | flops | bytes accessed | tf_op | source)
XLA Modules:
  0.0 136.8 jit_solution(17787697863340303887)
XLA Ops:
  0.6 1.5 %copy.18 = bf16[4,8,2,4,128]{4,3,2,1,0:T(4,128)(2,1)} copy(bf16[4,8,2,4,128]{4,1,0,2,3:T(8,128)(2,1)} %bitcast.14) | data formatting | bytes 131072 | tf_op jit(solution)/shard_map/transpose | solution.py:754
  2.2 0.0 copy-start
  2.2 0.0 copy-start.1
  2.2 3.9 %copy.24 = bf16[2,128,4,8,128]{4,1,3,2,0:T(8,128)(2,1)} copy(bf16[2,128,4,8,128]{4,3,2,1,0:T(8,128)(2,1)} %param.17) | data formatting | bytes 4194304 | tf_op args[5]
  6.0 0.0 copy-done
  6.0 0.0 copy-done.1
  6.0 2.7 %copy_bitcast_fusion.1 = (bf16[2,4,1024,128]{3,2,1,0:T(8,128)(2,1)}, bf16[2,4,1024,128]{3,2,1,0:T(8,128)(2,1)}) fusion(bf16[2,1024,4,128]{3,2,1,0:T(4,128)(2,1)S(1)} %copy-done, bf16[2,1024,4,128]{3,2,1,0:T(4,128)(2,1)S(1)} %copy-done.1), kind=kLoop, calls=%fused_computation.1 | loop fusion | bytes 8388608 | tf_op jit(solution)/shard_map/transpose | solution.py:748
  8.7 123.3 %shard_map.139 = (bf16[256,512]{1,0:T(8,128)(2,1)}, bf16[256,512]{1,0:T(8,128)(2,1)}, bf16[8,512]{1,0:T(8,128)(2,1)}) custom-call(s32[2]{0:T(128)} %phase_ref.1, s32[2,16]{1,0:T(2,128)} %ratio_ref.1, s32[2,16]{1,0:T(2,128)} %rlen_ref.1, bf16[2,4,1024,128]{3,2,1,0:T(8,128)(2,1)} %get-tuple-element.10.k_hbm, bf16[2,4,1024,128]{3,2,1,0:T(8,128)(2,1)} %get-tuple-element.9.v_hbm, ...), custom_call_target="tpu_custom_call" | custom-call | tf_op jit(solution)/shard_map/pallas_call | solution.py:690
  132.0 1.7 %reshape.19 = bf16[2,128,4,128]{3,2,1,0:T(4,128)(2,1)} reshape(bf16[256,512]{1,0:T(8,128)(2,1)} %get-tuple-element.6) | data formatting | bytes 524288 | tf_op jit(solution)/shard_map/reshape | solution.py:758
  133.7 0.7 reshape.21
  134.4 0.6 copy.25
  135.1 1.7 %reshape.20 = bf16[2,128,4,128]{3,2,1,0:T(4,128)(2,1)} reshape(bf16[256,512]{1,0:T(8,128)(2,1)} %get-tuple-element.7) | data formatting | bytes 524288 | tf_op jit(solution)/shard_map/reshape | solution.py:759
Async XLA Ops:
  2.2 3.9 %copy-start = (bf16[2,1024,4,128]{3,2,1,0:T(4,128)(2,1)S(1)}, bf16[2,1024,4,128]{3,2,1,0:T(4,128)(2,1)}, u32[]{:S(2)}) copy-start(bf16[2,1024,4,128]{3,2,1,0:T(4,128)(2,1)} %param.13) | copy-start | bytes 6291460
  2.2 3.9 %copy-start.1 = (bf16[2,1024,4,128]{3,2,1,0:T(4,128)(2,1)S(1)}, bf16[2,1024,4,128]{3,2,1,0:T(4,128)(2,1)}, u32[]{:S(2)}) copy-start(bf16[2,1024,4,128]{3,2,1,0:T(4,128)(2,1)} %param.12) | copy-start | bytes 6291460
